TPU v7x, 32 devices: a whole 2x2x4 slice. The times are simulated.
32 devices in a mesh: seq: 8 (over z, y), head: 4 (over x, core).
Axes of the slice: x: 2, y: 2, z: 4, core: 2. Of those that a mesh axis runs over, the one named last changes fastest.
Arguments:
- block_in: bfloat16 [1, 2048, 1024], P(None, 'seq'), may hold values from -6 to 6
- upstream: bfloat16 [1, 2048, 1024], P(None, 'seq'), may hold values from -6 to 6
- first_gain: float32 [1024], replicated, may hold values from 0.5 to 1.5
- project_in: bfloat16 [1024, 4, 512], P(None, 'head'), may hold values from -0.1875 to 0.1875
- filter_taps: float32 [4, 4, 512], P(None, 'head'), may hold values from -2 to 2
- squeeze: bfloat16 [1024, 16], replicated, may hold values from -0.1875 to 0.1875
- expand: bfloat16 [16, 512], P(None, 'head'), may hold values from -0.75 to 0.75
- decay_bias: float32 [512], P('head'), may hold values from 0 to 16
- gating: bfloat16 [1024, 1024], P(None, 'head'), may hold values from -0.1875 to 0.1875
- head_scale: float32 [256], replicated, may hold values from 0.5 to 1.5
- project_out: bfloat16 [1024, 1024], P('head'), may hold values from -0.375 to 0.375
- second_gain: float32 [1024], replicated, may hold values from 0.5 to 1.5
- hidden_gate: bfloat16 [1024, 2816], P(None, 'head'), may hold values from -0.1875 to 0.1875
- hidden_lift: bfloat16 [1024, 2816], P(None, 'head'), may hold values from -0.1875 to 0.1875
- hidden_drop: bfloat16 [2816, 1024], P('head'), may hold values from -0.15625 to 0.15625
Outputs:
- block_out: bfloat16 [1, 2048, 1024], P(None, 'seq')
- input_grad: float32 [1, 2048, 1024], P(None, 'seq')
- grad_first: float32 [1024], replicated
- grad_project: float32 [1024, 4, 512], P('seq', 'head')
- grad_taps: float32 [4, 4, 512], P(None, 'head')
- grad_squeeze: float32 [1024, 16], replicated
- grad_expand: float32 [16, 512], P(None, 'head')
- grad_bias: float32 [512], P('head')
- grad_gating: float32 [1024, 1024], P('seq', 'head')
- grad_scale: float32 [256], replicated
- grad_output: float32 [1024, 1024], P('head', 'seq')
- grad_second: float32 [1024], replicated
- grad_gate: float32 [1024, 2816], P('seq', 'head')
- grad_lift: float32 [1024, 2816], P('seq', 'head')
- grad_drop: float32 [2816, 1024], P('head', 'seq')
All inputs are finite; a program needn't handle non-finite values.
Results may differ from a plain program's by a relative error of at most 0.02.
Values sent between devices are 32-bit elements; how exact they have to be, the bound alone decides.
A program may use at most 128 MiB of HBM per device.

v0:
```python
import jax
import jax.numpy as jnp
from jax import lax
from jax.sharding import PartitionSpec as P

GROUP = 64
EPS = 1e-05
NORMALIZER = 16.0
HIGH = lax.Precision.HIGHEST


def shifted(x, axis, by):
    size = lax.axis_size(axis)
    pairs = [(i, i + by) for i in range(size) if 0 <= i + by < size]
    return lax.ppermute(x, axis, pairs)


def entering(value, axis, join, neutral, backward):
    count, mine = (lax.axis_size(axis), lax.axis_index(axis))
    pieces = jax.tree.map(lambda part: lax.all_gather(part, axis), value)
    if backward:
        pieces = jax.tree.map(lambda part: part[::-1], pieces)
        mine = count - 1 - mine
    total = jax.tree.map(
        lambda part, zero: jnp.full_like(part, 0) + jnp.asarray(zero, part.dtype), value, neutral
    )

    def lap(position, total):
        longer = join(total, jax.tree.map(lambda part: part[position], pieces))
        return jax.tree.map(lambda new, old: jnp.where(position < mine, new, old), longer, total)

    return lax.fori_loop(0, count - 1, lap, total)


def product(left, right):
    return jnp.dot(left, right, preferred_element_type=jnp.float32)


def against(left, right):
    return lax.dot_general(
        left, right, (((1,), (1,)), ((), ())), preferred_element_type=jnp.float32
    )


def across(left, right):
    return lax.dot_general(
        left, right, (((0,), (0,)), ((), ())), preferred_element_type=jnp.float32
    )


def rms_scale(values):
    return lax.rsqrt(jnp.mean(values * values, axis=-1, keepdims=True) + EPS)


def rms_back(values, scale, gain, incoming):
    weighted = gain * incoming
    cube = scale * scale * scale
    return scale * weighted - values * cube * jnp.mean(values * weighted, axis=-1, keepdims=True)


def silu_grad(values):
    logistic = jax.nn.sigmoid(values)
    return logistic * (1.0 + values * (1.0 - logistic))


def causal_mask(size):
    rows = lax.broadcasted_iota(jnp.int32, (size, size), 0)
    columns = lax.broadcasted_iota(jnp.int32, (size, size), 1)
    return (columns <= rows).astype(jnp.float32)


def chain(earlier, later):
    return (earlier[0] * later[0], later[0][..., None] * earlier[1] + later[1])


def grouped(array, seqs, count):
    return array.reshape((seqs, count, GROUP) + array.shape[2:])


def local_states(decays, updates, backward):

    def step(carry, item):
        decay, update = item
        return (jnp.exp(decay)[..., None] * carry + update, carry)

    init = jnp.zeros_like(updates[:, 0])
    total, states = lax.scan(
        step, init, (jnp.moveaxis(decays, 1, 0), jnp.moveaxis(updates, 1, 0)), reverse=backward
    )
    return (jnp.moveaxis(states, 0, 1), total)


def body(
    block_in,
    upstream,
    first_gain,
    project_in,
    filter_taps,
    squeeze,
    expand,
    decay_bias,
    gating,
    head_scale,
    project_out,
    second_gain,
    hidden_gate,
    hidden_lift,
    hidden_drop,
):
    seqs, tokens, width = block_in.shape
    total_rows = seqs * tokens
    key_dim = expand.shape[1]
    value_dim = gating.shape[1]
    mixed_dim = project_in.shape[2]
    lags = filter_taps.shape[0] - 1
    count = tokens // GROUP
    taps = filter_taps.reshape(lags + 1, mixed_dim)
    weight_in = project_in.reshape(width, mixed_dim)
    residual_in = block_in.reshape(total_rows, width).astype(jnp.float32)
    scale_one = rms_scale(residual_in)
    normed_one = (residual_in * scale_one * first_gain).astype(jnp.bfloat16)
    projected = product(normed_one, weight_in).reshape(seqs, tokens, mixed_dim)
    before = shifted(projected[:, tokens - lags :], "seq", 1)
    padded = jnp.concatenate([before, projected], axis=1)
    filtered = taps[0] * projected
    for lag in range(1, lags + 1):
        filtered = filtered + taps[lag] * padded[:, lags - lag : lags - lag + tokens]
    activated_low = jax.nn.silu(filtered).astype(jnp.bfloat16)
    activated = lax.optimization_barrier(activated_low).astype(jnp.float32)
    root = key_dim ** (-0.5)
    query = grouped(activated[..., :key_dim] * root, seqs, count)
    keys = grouped(activated[..., key_dim : 2 * key_dim], seqs, count)
    values = grouped(activated[..., 2 * key_dim :], seqs, count)
    squeezed = product(normed_one, squeeze).astype(jnp.bfloat16)
    logits = product(squeezed, expand) + decay_bias
    log_decay = grouped(
        (jax.nn.log_sigmoid(logits) / NORMALIZER).reshape(seqs, tokens, key_dim), seqs, count
    )
    gate_in = product(normed_one, gating)
    mask = causal_mask(GROUP)
    running = jnp.einsum("ij,snjc->snic", mask, log_decay, precision=HIGH)
    last = running[:, :, -1]
    query_in = query * jnp.exp(running)
    key_in = keys * jnp.exp(-running)
    key_end = keys * jnp.exp(last[:, :, None] - running)
    scores = jnp.einsum("snic,snjc->snij", query_in, key_in, precision=HIGH) * mask
    updates = jnp.einsum("snjc,snjd->sncd", key_end, values, precision=HIGH)
    starts_zero, state_total = local_states(last, updates, False)
    decay_sum = jnp.sum(last, axis=1)
    decay_total = jnp.exp(decay_sum)
    identity = (jnp.ones_like(decay_total), jnp.zeros_like(state_total))
    incoming = entering((decay_total, state_total), "seq", chain, identity, False)[1]
    before_group = jnp.cumsum(last, axis=1) - last
    starts = starts_zero + jnp.exp(before_group)[..., None] * incoming[:, None]
    mixed = jnp.einsum("snij,snjd->snid", scores, values, precision=HIGH)
    mixed = mixed + jnp.einsum("snic,sncd->snid", query_in, starts, precision=HIGH)
    mixed = mixed.reshape(total_rows, value_dim)
    scale_head = rms_scale(mixed)
    normed_head = mixed * scale_head * head_scale
    gated = (normed_head * jax.nn.silu(gate_in)).astype(jnp.bfloat16)
    branch = lax.psum(product(gated, project_out), "head")
    residual = residual_in + branch
    scale_two = rms_scale(residual)
    normed_two = (residual * scale_two * second_gain).astype(jnp.bfloat16)
    gate_value = product(normed_two, hidden_gate)
    lift_value = product(normed_two, hidden_lift)
    inner = (jax.nn.silu(gate_value) * lift_value).astype(jnp.bfloat16)
    feed = lax.psum(product(inner, hidden_drop), "head")
    block_out = (residual + feed).astype(jnp.bfloat16).reshape(seqs, tokens, width)
    seed = upstream.reshape(total_rows, width)
    grad_drop = across(inner, seed)
    grad_inner = against(seed, hidden_drop)
    grad_gv = (grad_inner * lift_value * silu_grad(gate_value)).astype(jnp.bfloat16)
    grad_lv = (grad_inner * jax.nn.silu(gate_value)).astype(jnp.bfloat16)
    grad_gate = across(normed_two, grad_gv)
    grad_lift = across(normed_two, grad_lv)
    feed_grads = (
        lax.psum_scatter(grad_gate, "seq", scatter_dimension=0, tiled=True),
        lax.psum_scatter(grad_lift, "seq", scatter_dimension=0, tiled=True),
        lax.psum_scatter(grad_drop, "seq", scatter_dimension=1, tiled=True),
    )
    grad_two = lax.psum(against(grad_gv, hidden_gate) + against(grad_lv, hidden_lift), "head")
    grad_second = jnp.sum(grad_two * residual * scale_two, axis=0)
    grad_resid = seed.astype(jnp.float32) + rms_back(residual, scale_two, second_gain, grad_two)
    resid_low = grad_resid.astype(jnp.bfloat16)
    grad_output = across(gated, resid_low)
    grad_gated = against(resid_low, project_out)
    grad_gatein = (grad_gated * normed_head * silu_grad(gate_in)).astype(jnp.bfloat16)
    grad_normhead = grad_gated * jax.nn.silu(gate_in)
    grad_scale = jnp.sum(grad_normhead * mixed * scale_head, axis=0)
    grad_mixed_low = rms_back(mixed, scale_head, head_scale, grad_normhead).astype(jnp.bfloat16)
    grad_mixed = lax.optimization_barrier(grad_mixed_low).astype(jnp.float32)
    outgrad = grouped(grad_mixed.reshape(seqs, tokens, value_dim), seqs, count)
    query_end = jnp.einsum("snic,snid->sncd", query_in, outgrad, precision=HIGH)
    following_zero, back_total = local_states(last, query_end, True)
    after = entering((decay_total, back_total), "seq", chain, identity, True)[1]
    after_group = decay_sum[:, None] - jnp.cumsum(last, axis=1)
    following = following_zero + jnp.exp(after_group)[..., None] * after[:, None]
    inner_group = jnp.einsum("snid,snjd->snij", outgrad, values, precision=HIGH) * mask
    grad_query = jnp.exp(running) * (
        jnp.einsum("snij,snjc->snic", inner_group, key_in, precision=HIGH)
        + jnp.einsum("snid,sncd->snic", outgrad, starts, precision=HIGH)
    )
    grad_keys = jnp.exp(-running) * jnp.einsum(
        "snij,snic->snjc", inner_group, query_in, precision=HIGH
    )
    grad_keys = grad_keys + jnp.exp(last[:, :, None] - running) * jnp.einsum(
        "snjd,sncd->snjc", values, following, precision=HIGH
    )
    grad_values = jnp.einsum("snij,snid->snjd", scores, outgrad, precision=HIGH)
    grad_values = grad_values + jnp.einsum("snjc,sncd->snjd", key_end, following, precision=HIGH)
    grad_running = (query * grad_query - keys * grad_keys).reshape(seqs, tokens, key_dim)
    state_end = decay_total[..., None] * incoming + state_total
    beyond = jnp.sum(state_end * after, axis=-1)
    upper = jnp.transpose(causal_mask(tokens))
    suffix = jnp.einsum("ij,sjc->sic", upper, grad_running, precision=HIGH)
    grad_log = suffix + beyond[:, None]
    grad_act = jnp.concatenate(
        [
            grad_query.reshape(seqs, tokens, key_dim) * root,
            grad_keys.reshape(seqs, tokens, key_dim),
            grad_values.reshape(seqs, tokens, value_dim),
        ],
        axis=-1,
    )
    grad_filtered = grad_act * silu_grad(filtered)
    later = shifted(grad_filtered[:, :lags], "seq", -1)
    padded_back = jnp.concatenate([grad_filtered, later], axis=1)
    grad_projected = taps[0] * grad_filtered
    tap_rows = [jnp.sum(grad_filtered * projected, axis=(0, 1))]
    for lag in range(1, lags + 1):
        grad_projected = grad_projected + taps[lag] * padded_back[:, lag : lag + tokens]
        tap_rows.append(
            jnp.sum(grad_filtered * padded[:, lags - lag : lags - lag + tokens], axis=(0, 1))
        )
    grad_taps = jnp.stack(tap_rows).reshape(lags + 1, 1, mixed_dim)
    grad_projected = grad_projected.reshape(total_rows, mixed_dim).astype(jnp.bfloat16)
    grad_logits = grad_log.reshape(total_rows, key_dim) * jax.nn.sigmoid(-logits) / NORMALIZER
    grad_bias = jnp.sum(grad_logits, axis=0)
    logits_low = grad_logits.astype(jnp.bfloat16)
    grad_expand = across(squeezed, logits_low)
    squeeze_low = against(logits_low, expand).astype(jnp.bfloat16)
    grad_squeeze = across(normed_one, squeeze_low)
    grad_project = across(normed_one, grad_projected).reshape(width, 1, mixed_dim)
    grad_gating = across(normed_one, grad_gatein)
    partial_value = (
        against(grad_projected, weight_in)
        + against(grad_gatein, gating)
        + against(squeeze_low, squeeze)
    )
    grad_one = lax.psum(partial_value, "head")
    grad_first = jnp.sum(grad_one * residual_in * scale_one, axis=0)
    input_grad = (grad_resid + rms_back(residual_in, scale_one, first_gain, grad_one)).reshape(
        seqs, tokens, width
    )
    mixer_grads = (
        lax.psum_scatter(grad_project, "seq", scatter_dimension=0, tiled=True),
        lax.psum_scatter(grad_gating, "seq", scatter_dimension=0, tiled=True),
        lax.psum_scatter(grad_output, "seq", scatter_dimension=1, tiled=True),
    )
    summed = tuple(mixer_grads) + tuple(feed_grads)
    small_head = lax.psum((grad_taps, grad_expand, grad_bias, grad_first, grad_second), "seq")
    shared = lax.psum((grad_scale, grad_squeeze), ("seq", "head"))
    return (
        block_out,
        input_grad,
        small_head[3],
        summed[0],
        small_head[0],
        shared[1],
        small_head[1],
        small_head[2],
        summed[1],
        shared[0],
        summed[2],
        small_head[4],
        summed[3],
        summed[4],
        summed[5],
    )


def solution(mesh):
    in_specs = (
        P(None, "seq", None),
        P(None, "seq", None),
        P(),
        P(None, "head", None),
        P(None, "head", None),
        P(),
        P(None, "head"),
        P("head"),
        P(None, "head"),
        P(),
        P("head", None),
        P(),
        P(None, "head"),
        P(None, "head"),
        P("head", None),
    )
    out_specs = (
        P(None, "seq", None),
        P(None, "seq", None),
        P(),
        P("seq", "head", None),
        P(None, "head", None),
        P(),
        P(None, "head"),
        P("head"),
        P("seq", "head"),
        P(),
        P("head", "seq"),
        P(),
        P("seq", "head"),
        P("seq", "head"),
        P("head", "seq"),
    )
    return jax.shard_map(body, mesh=mesh, in_specs=in_specs, out_specs=out_specs, check_vma=False)
```

profile of v0, /device:TPU:0, one launch (start us, length us, event | category | flops | bytes accessed | tf_op | source)
XLA Modules:
  0.0 871.2 jit_solution(14256679517528602044)
XLA Ops:
  7.3 1.3 fusion.21
  9.2 1.9 fusion.35
  11.2 4.9 collective-permute-start
  17.5 1.1 multiply_convert_fusion.4
  19.1 1.2 convolution_bitcast_fusion.2
  20.4 4.3 while.58
  20.4 1.0 bitcast_add_fusion.13
  21.5 1.0 bitcast_add_fusion.13
  22.6 1.0 bitcast_add_fusion.13
  26.0 21.5 %all-gather.3 = f32[8,1,128]{2,1,0:T(1,128)S(1)} all-gather(f32[1,1,128]{2,1,0:T(1,128)S(1)} %get-tuple-element.555), channel_id=2, replica_groups=mesh['seq'=8,'head'=4] {'seq'}, dimensions={0}, use_global_device_ids=true | all-gather | bytes 4608 | tf_op jit(solution)/shard_map/all_gather | solution.py:20
  49.4 18.3 %all-gather.7.cloned.1.call-done = f32[8,128,256]{2,1,0:T(8,128)} async-done(((f32[1,128,256]{2,1,0:T(8,128)}), f32[8,128,256]{2,1,0:T(8,128)}) %all-gather.7.cloned.1.call-update) | async-done | bytes 1048592 | tf_op jit(solution)/shard_map/all_gather | solution.py:20
  67.7 7.3 while.59
  75.6 1.6 multiply_reduce_fusion.7
  77.3 2.2 multiply_convert_fusion.6
  79.4 1.3 fusion.118
  80.8 35.1 %all-reduce.7.cloned.1.call-done = f32[256,1024]{1,0:T(8,128)} async-done(((f32[256,1024]{1,0:T(8,128)}), f32[256,1024]{1,0:T(8,128)}) %all-reduce.7.cloned.1.call-update) | async-done | bytes 1048592 | tf_op jit(solution)/shard_map/psum | solution.py:161
  115.9 1.4 multiply_reduce_fusion.2
  121.3 1.5 multiply_convert_fusion.1
  123.6 1.6 convolution_add_fusion.2
  125.3 1.2 multiply_multiply_fusion.1
  126.5 35.6 %all-reduce.9.cloned.1.call-done = f32[256,1024]{1,0:T(8,128)} async-done(((f32[256,1024]{1,0:T(8,128)}), f32[256,1024]{1,0:T(8,128)}) %all-reduce.9.cloned.1.call-update) | async-done | bytes 1048592 | tf_op jit(solution)/shard_map/psum | solution.py:182
  162.1 2.2 multiply_reduce_fusion
  164.4 1.1 subtract_add_fusion
  165.6 1.6 fusion.65
  168.0 1.2 convolution_bitcast_fusion.1
  170.1 9.2 %while.60 = (s32[]{:T(128)}, f32[1,128,256]{2,1,0:T(8,128)S(1)}, f32[4,1,128,256]{3,2,1,0:T(8,128)}, f32[4,1,128]{2,1,0:T(1,128)}, f32[4,1,128,256]{3,2,1,0:T(8,128)}, /*index=5*/s32[]{:T(128)}, s32[]{:T(128)}, s32[]{:T(128)}) while((s32[]{:T(128)}, f32[1,128,256]{2,1,0:T(8,128)S(1)}, f32[4,1,128,256]{3,2,1,0:T(8,128)}, ...), condition=%wide.region_15.16_spmd.clone, body=%wide.region_14.15_spmd.clone.sunk | while | flops 131076 | bytes 657016 | solution.py:87
  180.9 2.6 fusion.121
  183.7 1.0 fusion.16
  185.1 1.0 fusion.123
  186.1 1.2 fusion.15
  187.3 33.6 %all-gather.9.cloned.1.call-done = f32[8,128,256]{2,1,0:T(8,128)} async-done(((f32[1,128,256]{2,1,0:T(8,128)}), f32[8,128,256]{2,1,0:T(8,128)}) %all-gather.9.cloned.1.call-update) | async-done | bytes 1048592 | tf_op jit(solution)/shard_map/all_gather | solution.py:20
  220.9 2.3 reverse_bitcast_fusion
  223.2 15.3 %while.61 = (s32[]{:T(128)}, f32[1,128,256]{2,1,0:T(8,128)S(1)}, s32[]{:T(128)}, f32[8,1,128]{2,1,0:T(1,128)}, f32[8,1,128,256]{3,2,1,0:T(8,128)}, /*index=5*/s32[]{:T(128)}, s32[]{:T(128)}) while((s32[]{:T(128)}, f32[1,128,256]{2,1,0:T(8,128)S(1)}, s32[]{:T(128)}, f32[8,1,128]{2,1,0:T(1,128)}, f32[8,1,128,256]{3,2,1,0:T(8,128)}, ...), condition=%wide.region_17.18_spmd.clone, body=%wide.region_16.17_spmd.clone.sunk | while | flops 131076 | bytes 394857 | solution.py:32
  223.2 1.2 dynamic-slice_bitcast_fusion.5
  225.4 1.2 dynamic-slice_bitcast_fusion.5
  227.6 1.2 dynamic-slice_bitcast_fusion.5
  229.8 1.2 dynamic-slice_bitcast_fusion.5
  232.0 1.2 dynamic-slice_bitcast_fusion.5
  234.2 1.2 dynamic-slice_bitcast_fusion.5
  236.4 1.2 dynamic-slice_bitcast_fusion.5
  239.5 1.8 convolution_add_fusion.3
  242.0 1.0 multiply_reduce_fusion.5
  243.0 1.4 collective-permute-start.1
  246.1 2.6 collective-permute-done.1
  250.2 1.3 convolution_add_fusion
  251.6 1.9 convolution_bitcast_fusion
  254.5 2.6 fusion.70
  257.2 2.4 fusion.105
  259.6 3.1 fusion.124
  262.8 3.2 fusion.125
  267.0 3.2 fusion.51
  270.8 38.8 %psum.86 = f32[256]{0:T(256)} all-reduce(f32[256]{0:T(256)S(1)} %copy-done.89), channel_id=1, replica_groups=mesh['seq'=8,'head'=4] {'seq','head'}, use_global_device_ids=true, to_apply=%region_35.36 | all-reduce | flops 256 | bytes 2048 | tf_op jit(solution)/shard_map/psum | solution.py:263
  309.9 1.5 fusion.30
  311.4 37.7 %all-reduce = (f32[1024]{0:T(1024)}, f32[4,1,512]{2,1,0:T(1,128)}, f32[16,128]{1,0:T(8,128)}, f32[128]{0:T(128)}, f32[1024]{0:T(1024)}) all-reduce(f32[1024]{0:T(1024)S(1)} %get-tuple-element.475, f32[4,1,512]{2,1,0:T(1,128)S(1)} %reshape.447, f32[16,128]{1,0:T(8,128)S(1)} %fusion.99, ...), channel_id=1, replica_groups=mesh['seq'=8,'head'=4] {'seq'}, use_global_device_ids=true, to_apply=%region_22.23 | all-reduce | flops 6272 | bytes 50176 | tf_op jit(solution)/shard_map/psum | solution.py:262
  349.1 3.4 fusion.27
  352.5 21.5 %reduce-scatter.7.cloned.1.call-done = f32[128,1,512]{2,0,1:T(8,128)} async-done(((f32[1024,1,512]{2,0,1:T(8,128)}), f32[128,1,512]{2,0,1:T(8,128)}) %reduce-scatter.7.cloned.1.call-update) | async-done | bytes 262160 | tf_op jit(solution)/shard_map/reduce_scatter | solution.py:257
  374.1 1.9 copy.47
  376.0 122.0 %all-reduce.11.cloned.1.call-done = f32[1024,16]{0,1:T(8,128)} async-done(((f32[1024,16]{0,1:T(8,128)}), f32[1024,16]{0,1:T(8,128)}) %all-reduce.11.cloned.1.call-update) | async-done | bytes 65552 | tf_op jit(solution)/shard_map/psum | solution.py:263
  498.0 69.9 %reduce-scatter.11.cloned.1.call-done = f32[256,128]{1,0:T(8,128)} async-done(((f32[256,1024]{1,0:T(8,128)}), f32[256,128]{1,0:T(8,128)}) %reduce-scatter.11.cloned.1.call-update) | async-done | bytes 131088 | tf_op jit(solution)/shard_map/reduce_scatter | solution.py:259
  567.9 67.2 %reduce-scatter.9.cloned.1.call-done = f32[128,256]{1,0:T(8,128)} async-done(((f32[1024,256]{1,0:T(8,128)}), f32[128,256]{1,0:T(8,128)}) %reduce-scatter.9.cloned.1.call-update) | async-done | bytes 131088 | tf_op jit(solution)/shard_map/reduce_scatter | solution.py:258
  635.2 75.6 %reduce-scatter.13.cloned.1.call-done = f32[128,704]{0,1:T(8,128)} async-done(((f32[1024,704]{0,1:T(8,128)}), f32[128,704]{0,1:T(8,128)}) %reduce-scatter.13.cloned.1.call-update) | async-done | bytes 360464 | tf_op jit(solution)/shard_map/reduce_scatter | solution.py:178
  710.8 76.2 %reduce-scatter.15.cloned.1.call-done = f32[128,704]{0,1:T(8,128)} async-done(((f32[1024,704]{0,1:T(8,128)}), f32[128,704]{0,1:T(8,128)}) %reduce-scatter.15.cloned.1.call-update) | async-done | bytes 360464 | tf_op jit(solution)/shard_map/reduce_scatter | solution.py:179
  787.0 75.9 %reduce-scatter.17.cloned.1.call-done = f32[704,128]{1,0:T(8,128)} async-done(((f32[704,1024]{1,0:T(8,128)}), f32[704,128]{1,0:T(8,128)}) %reduce-scatter.17.cloned.1.call-update) | async-done | bytes 360464 | tf_op jit(solution)/shard_map/reduce_scatter | solution.py:180
  862.9 1.5 copy.89
  (303 shorter events, 46.7 us)
Async XLA Ops:
  7.2 113.7 %copy-start = (bf16[704,1024]{1,0:T(8,128)(2,1)S(1)}, bf16[704,1024]{1,0:T(8,128)(2,1)}, u32[]{:S(2)}) copy-start(bf16[704,1024]{1,0:T(8,128)(2,1)} %param.37) | copy-start | bytes 4325380
  7.2 8.9 %copy-start.3 = (bf16[1,256,1024]{2,1,0:T(8,128)(2,1)S(1)}, bf16[1,256,1024]{2,1,0:T(8,128)(2,1)}, u32[]{:S(2)}) copy-start(bf16[1,256,1024]{2,1,0:T(8,128)(2,1)} %param.23) | copy-start | bytes 1572868
  7.2 8.9 %copy-start.53 = (f32[1024]{0:T(1024)S(1)}, f32[1024]{0:T(1024)}, u32[]{:S(2)}) copy-start(f32[1024]{0:T(1024)} %param.25) | copy-start | bytes 12292
  7.2 8.9 %copy-start.55 = (bf16[1024,16]{0,1:T(8,128)(2,1)S(1)}, bf16[1024,16]{0,1:T(8,128)(2,1)}, u32[]{:S(2)}) copy-start(bf16[1024,16]{0,1:T(8,128)(2,1)} %param.28) | copy-start | bytes 98308
  7.2 60.5 %all-gather.7.cloned.1.call-start = ((), (), s32[]{:S(2)}) async-start(), calls=%async_computation.15 | async-start | bytes 1179648 | tf_op jit(solution)/shard_map/all_gather | solution.py:20
  9.2 7.2 copy-start.83
  9.2 7.2 copy-start.91
  9.2 8.2 copy-start.81
  11.2 7.5 copy-start.8
  11.2 6.3 collective-permute-start
  18.7 49.0 %copy-start.12 = (f32[1,256,128]{2,1,0:T(8,128)}, f32[1,256,128]{2,1,0:T(8,128)S(1)}, u32[]{:S(2)}) copy-start(f32[1,256,128]{2,1,0:T(8,128)S(1)} %slice.81) | copy-start | bytes 393220
  18.8 29.7 %copy-start.19 = (bf16[1,256,256]{2,1,0:T(8,128)(2,1)}, bf16[1,256,256]{2,1,0:T(8,128)(2,1)S(1)}, u32[]{:S(2)}) copy-start(bf16[1,256,256]{2,1,0:T(8,128)(2,1)S(1)} %slice.82) | copy-start | bytes 393220
  19.1 148.3 %copy-start.24 = (f32[1,4,64,128]{3,2,1,0:T(8,128)}, f32[1,4,64,128]{3,2,1,0:T(8,128)S(1)}, u32[]{:S(2)}) copy-start(f32[1,4,64,128]{3,2,1,0:T(8,128)S(1)} %get-tuple-element.558) | copy-start | bytes 393220
  24.7 50.9 %copy-start.16 = (f32[4,1,128,256]{3,2,1,0:T(8,128)}, f32[4,1,128,256]{3,2,1,0:T(8,128)S(1)}, u32[]{:S(2)}) copy-start(f32[4,1,128,256]{3,2,1,0:T(8,128)S(1)} %get-tuple-element.335) | copy-start | bytes 1572868
  25.3 90.6 %all-reduce.7.cloned.1.call-start = ((), (), s32[]{:S(2)}) async-start(), calls=%async_computation.6 | async-start | bytes 2097152 | tf_op jit(solution)/shard_map/psum | solution.py:161
  25.4 42.3 %copy-start.47 = (f32[64,64]{1,0:T(8,128)}, f32[64,64]{1,0:T(8,128)S(1)}, u32[]{:S(2)}) copy-start(f32[64,64]{1,0:T(8,128)S(1)} %fusion.102) | copy-start | bytes 49156
  48.1 27.5 %copy-start.60 = (f32[4,128]{1,0:T(4,128)}, f32[4,128]{1,0:T(4,128)S(1)}, u32[]{:S(2)}) copy-start(f32[4,128]{1,0:T(4,128)S(1)} %get-tuple-element.549) | copy-start | bytes 6148
  48.5 28.7 %copy-start.34 = (f32[4,64,64]{2,1,0:T(8,128)}, f32[4,64,64]{2,1,0:T(8,128)S(1)}, u32[]{:S(2)}) copy-start(f32[4,64,64]{2,1,0:T(8,128)S(1)} %convolution_multiply_fusion.1) | copy-start | bytes 196612
  67.7 9.6 %copy-start.87 = (f32[256]{0:T(256)S(1)}, f32[256]{0:T(256)}, u32[]{:S(2)}) copy-start(f32[256]{0:T(256)} %param.32) | copy-start | bytes 3076
  80.7 37.2 %copy-start.54 = (f32[1024]{0:T(1024)S(1)}, f32[1024]{0:T(1024)}, u32[]{:S(2)}) copy-start(f32[1024]{0:T(1024)} %param.34) | copy-start | bytes 12292
  80.8 81.4 %all-reduce.9.cloned.1.call-start = ((), (), s32[]{:S(2)}) async-start(), calls=%async_computation.7 | async-start | bytes 2097152 | tf_op jit(solution)/shard_map/psum | solution.py:182
  125.2 95.7 %all-gather.9.cloned.1.call-start = ((), (), s32[]{:S(2)}) async-start(), calls=%async_computation.16 | async-start | bytes 1179648 | tf_op jit(solution)/shard_map/all_gather | solution.py:20
  170.1 10.1 %copy-start.73 = (f32[8,1,128]{2,1,0:T(1,128)S(1)}, f32[8,1,128]{2,1,0:T(1,128)}, u32[]{:S(2)}) copy-start(f32[8,1,128]{2,1,0:T(1,128)} %copy-done.72) | copy-start | bytes 12292
  180.0 3.5 copy-start.20
  180.0 129.8 %all-reduce.13.cloned.1.call-start = ((), (), s32[]{:S(2)}) async-start(), calls=%async_computation.17 | async-start | bytes 4194304 | tf_op jit(solution)/shard_map/psum | solution.py:168
  180.9 2.6 copy-start.23
  180.9 2.6 copy-start.48
  180.9 2.9 copy-start.25
  180.9 3.9 copy-start.13
  183.5 2.6 copy-start.17
  183.5 2.6 copy-start.61
  223.2 15.4 %copy-start.2 = (f32[1,128,256]{2,1,0:T(8,128)S(1)}, f32[1,128,256]{2,1,0:T(8,128)}, u32[]{:S(2)}) copy-start(f32[1,128,256]{2,1,0:T(8,128)} %copy-done.1) | copy-start | bytes 393220
  223.2 16.3 %copy-start.59 = (f32[4,128]{1,0:T(4,128)S(1)}, f32[4,128]{1,0:T(4,128)}, u32[]{:S(2)}) copy-start(f32[4,128]{1,0:T(4,128)} %get-tuple-element.548) | copy-start | bytes 6148
  238.6 2.8 copy-start.14
  238.6 2.8 copy-start.15
  238.6 2.8 copy-start.21
  238.6 2.8 copy-start.33
  238.6 2.8 copy-start.39
  238.6 2.8 copy-start.40
  241.9 2.5 copy-start.92
  242.0 4.0 copy-start.84
  242.0 6.7 copy-start.63
  242.0 6.7 copy-start.65
  242.0 6.7 copy-start.67
  242.0 6.7 copy-start.69
  243.0 5.9 copy-start.38
  243.0 5.7 collective-permute-start.1
  246.1 3.4 copy-start.43
  246.1 3.4 copy-start.46
  251.5 122.5 %reduce-scatter.7.cloned.1.call-start = ((), (), s32[]{:S(2)}) async-start(), calls=%async_computation.8 | async-start | bytes 2359296 | tf_op jit(solution)/shard_map/reduce_scatter | solution.py:257
  253.5 244.6 %all-reduce.11.cloned.1.call-start = ((), (), s32[]{:S(2)}) async-start(), calls=%async_computation.9 | async-start | bytes 131072 | tf_op jit(solution)/shard_map/psum | solution.py:263
  254.5 313.5 %reduce-scatter.11.cloned.1.call-start = ((), (), s32[]{:S(2)}) async-start(), calls=%async_computation.11 | async-start | bytes 1179648 | tf_op jit(solution)/shard_map/reduce_scatter | solution.py:259
  257.1 378.0 %reduce-scatter.9.cloned.1.call-start = ((), (), s32[]{:S(2)}) async-start(), calls=%async_computation.10 | async-start | bytes 1179648 | tf_op jit(solution)/shard_map/reduce_scatter | solution.py:258
  259.6 451.2 %reduce-scatter.13.cloned.1.call-start = ((), (), s32[]{:S(2)}) async-start(), calls=%async_computation.12 | async-start | bytes 3244032 | tf_op jit(solution)/shard_map/reduce_scatter | solution.py:178
  262.7 524.2 %reduce-scatter.15.cloned.1.call-start = ((), (), s32[]{:S(2)}) async-start(), calls=%async_computation.13 | async-start | bytes 3244032 | tf_op jit(solution)/shard_map/reduce_scatter | solution.py:179
  266.0 596.9 %reduce-scatter.17.cloned.1.call-start = ((), (), s32[]{:S(2)}) async-start(), calls=%async_computation.14 | async-start | bytes 3244032 | tf_op jit(solution)/shard_map/reduce_scatter | solution.py:180
  270.2 39.5 %copy-start.76 = (f32[512]{0:T(512)S(1)}, f32[512]{0:T(512)}, u32[]{:S(2)}) copy-start(f32[512]{0:T(512)} %get-tuple-element.478) | copy-start | bytes 6148
  270.2 39.5 %copy-start.77 = (f32[512]{0:T(512)S(1)}, f32[512]{0:T(512)}, u32[]{:S(2)}) copy-start(f32[512]{0:T(512)} %get-tuple-element.479) | copy-start | bytes 6148
  270.2 39.5 %copy-start.78 = (f32[512]{0:T(512)S(1)}, f32[512]{0:T(512)}, u32[]{:S(2)}) copy-start(f32[512]{0:T(512)} %get-tuple-element.482) | copy-start | bytes 6148
  270.2 39.5 %copy-start.51 = (bf16[256,128]{1,0:T(8,128)(2,1)S(1)}, bf16[256,128]{1,0:T(8,128)(2,1)}, u32[]{:S(2)}) copy-start(bf16[256,128]{1,0:T(8,128)(2,1)} %copy-done.50) | copy-start | bytes 196612
  270.2 39.5 %copy-start.80 = (bf16[256,16]{0,1:T(8,128)(2,1)S(1)}, bf16[256,16]{0,1:T(8,128)(2,1)}, u32[]{:S(2)}) copy-start(bf16[256,16]{0,1:T(8,128)(2,1)} %copy-done.79) | copy-start | bytes 24580
  270.2 41.2 %copy-start.71 = (f32[1024]{0:T(1024)S(1)}, f32[1024]{0:T(1024)}, u32[]{:S(2)}) copy-start(f32[1024]{0:T(1024)} %get-tuple-element.473) | copy-start | bytes 12292
  270.2 41.2 %copy-start.90 = (f32[128]{0:T(128)S(1)}, f32[128]{0:T(128)}, u32[]{:S(2)}) copy-start(f32[128]{0:T(128)} %get-tuple-element.566) | copy-start | bytes 1540
  270.2 78.9 %copy-start.85 = (f32[256]{0:T(256)S(1)}, f32[256]{0:T(256)}, u32[]{:S(2)}) copy-start(f32[256]{0:T(256)} %get-tuple-element.550) | copy-start | bytes 3076
  (43 other events, 58.3 us)
Sparse Core Ops, SparseCore 0:
  25.4 42.2 all-gather.6
  80.9 34.9 all-reduce.6
  125.4 36.7 all-reduce.8
  180.1 40.7 all-gather.8
  251.6 50.4 all-reduce.12
  305.5 68.4 reduce-scatter.6
  379.6 118.3 all-reduce.10
  502.0 65.8 reduce-scatter.10
  571.9 63.1 reduce-scatter.8
  639.1 71.6 reduce-scatter.12
  714.9 71.9 reduce-scatter.14
  791.0 71.8 reduce-scatter.16
where the time goes:
time: 873 us; the launch traced here: 871 us
  waiting for transfers between devices  634 us (73%)
  blocking collectives  98 us (11%)
  matrix products  47.6 us (5%)
  other arithmetic  42.4 us (5%)
  local copies, waits for them, and re-layouts  26.4 us (3%)
  between operations  15.4 us (2%)
    psum x1, waiting for transfers between devices, body(): shared = lax.psum((grad_scale, grad_squeeze), ('seq', 'head'))  122 us
    reduce_scatter x1, waiting for transfers between devices, body(): lax.psum_scatter(grad_lift, 'seq', scatter_dimension=0, tiled=True)  76.2 us
    reduce_scatter x1, waiting for transfers between devices, body(): lax.psum_scatter(grad_drop, 'seq', scatter_dimension=1, tiled=True)  75.9 us
    reduce_scatter x1, waiting for transfers between devices, body(): lax.psum_scatter(grad_gate, 'seq', scatter_dimension=0, tiled=True)  75.6 us
    reduce_scatter x1, waiting for transfers between devices, body(): lax.psum_scatter(grad_output, 'seq', scatter_dimension=1, tiled=True)  69.9 us
    reduce_scatter x1, waiting for transfers between devices, body(): lax.psum_scatter(grad_gating, 'seq', scatter_dimension=0, tiled=True)  67.2 us
    all_gather x2, waiting for transfers between devices, entering(): pieces = jax.tree.map(lambda part: lax.all_gather(part, axis), value)  51.9 us
    psum x1, blocking collectives, body(): shared = lax.psum((grad_scale, grad_squeeze), ('seq', 'head'))  38.8 us
  transfers between devices with their start and end apart: 14, of which 12 were waited for; matrix products, arithmetic and copies ran while one was open for 4% of the time, Pallas kernels for 0%

commit v1 on v0

--- a/solution.py
+++ b/solution.py
@@ -260,7 +260,7 @@
     )
     summed = tuple(mixer_grads) + tuple(feed_grads)
     small_head = lax.psum((grad_taps, grad_expand, grad_bias, grad_first, grad_second), "seq")
-    shared = lax.psum((grad_scale, grad_squeeze), ("seq", "head"))
+    shared = lax.psum(lax.psum((grad_scale, grad_squeeze), axis_name="seq"), axis_name="head")
     return (
         block_out,
         input_grad,

time: 873 us -> 817 us (0.936)
  blocking collectives: 98 us -> 66 us
  waiting for transfers between devices: 634 us -> 606 us
    psum x1, waiting for transfers between devices: 122 us -> 61 us  [body(): lax.psum((grad_scale, grad_squeeze), axis_name='seq')]
    psum x1, waiting for transfers between devices: 0.01 us -> 35.4 us  [body(): feed = lax.psum(product(inner, hidden_drop), 'head')]
    psum x1, blocking collectives: 38.8 us -> 6.43 us  [body(): lax.psum(lax.psum((grad_scale, grad_squeeze), axis_name='seq'), axis_name...]
  transfers between devices with their start and end apart: 14 -> 14, of which waited for: 12 -> 13; matrix products, arithmetic and copies ran while one was open for 4% -> 5% of each run, Pallas kernels for 0% -> 0%
where the time goes in v1:
time: 817 us; the launch traced here: 815 us
  waiting for transfers between devices  606 us (74%)
  blocking collectives  66 us (8%)
  matrix products  48.8 us (6%)
  other arithmetic  44.4 us (5%)
  local copies, waits for them, and re-layouts  27.2 us (3%)
  between operations  15.3 us (2%)
    reduce_scatter x1, waiting for transfers between devices, body(): lax.psum_scatter(grad_lift, 'seq', scatter_dimension=0, tiled=True)  76.3 us
    reduce_scatter x1, waiting for transfers between devices, body(): lax.psum_scatter(grad_drop, 'seq', scatter_dimension=1, tiled=True)  76.1 us
    reduce_scatter x1, waiting for transfers between devices, body(): lax.psum_scatter(grad_gate, 'seq', scatter_dimension=0, tiled=True)  76 us
    reduce_scatter x1, waiting for transfers between devices, body(): lax.psum_scatter(grad_gating, 'seq', scatter_dimension=0, tiled=True)  67.1 us
    reduce_scatter x1, waiting for transfers between devices, body(): lax.psum_scatter(grad_output, 'seq', scatter_dimension=1, tiled=True)  65.8 us
    psum x1, waiting for transfers between devices, body(): lax.psum((grad_scale, grad_squeeze), axis_name='seq')  61 us
    all_gather x2, waiting for transfers between devices, entering(): pieces = jax.tree.map(lambda part: lax.all_gather(part, axis), value)  51.8 us
    psum x1, blocking collectives, body(): lax.psum((grad_taps, grad_expand, grad_bias, grad_first, grad_second), 's...  38 us
  transfers between devices with their start and end apart: 14, of which 13 were waited for; matrix products, arithmetic and copies ran while one was open for 5% of the time, Pallas kernels for 0%

profile of v1, /device:TPU:0, one launch (start us, length us, event | category | flops | bytes accessed | tf_op | source)
XLA Modules:
  0.0 815.3 jit_solution(5803230161805368193)
XLA Ops:
  7.3 1.3 fusion.21
  9.2 1.9 fusion.35
  11.2 4.9 collective-permute-start
  17.5 1.1 multiply_convert_fusion.4
  19.1 1.2 convolution_bitcast_fusion.2
  20.3 4.3 while.58
  20.4 1.0 bitcast_add_fusion.13
  26.0 21.5 %all-gather.3 = f32[8,1,128]{2,1,0:T(1,128)S(1)} all-gather(f32[1,1,128]{2,1,0:T(1,128)S(1)} %get-tuple-element.557), channel_id=2, replica_groups=mesh['seq'=8,'head'=4] {'seq'}, dimensions={0}, use_global_device_ids=true | all-gather | bytes 4608 | tf_op jit(solution)/shard_map/all_gather | solution.py:20
  49.5 18.2 %all-gather.7.cloned.1.call-done = f32[8,128,256]{2,1,0:T(8,128)} async-done(((f32[1,128,256]{2,1,0:T(8,128)}), f32[8,128,256]{2,1,0:T(8,128)}) %all-gather.7.cloned.1.call-update) | async-done | bytes 1048592 | tf_op jit(solution)/shard_map/all_gather | solution.py:20
  67.7 7.3 while.59
  75.6 1.6 multiply_reduce_fusion.7
  77.2 2.2 multiply_convert_fusion.6
  79.4 1.3 fusion.118
  80.8 35.1 %all-reduce.7.cloned.1.call-done = f32[256,1024]{1,0:T(8,128)} async-done(((f32[256,1024]{1,0:T(8,128)}), f32[256,1024]{1,0:T(8,128)}) %all-reduce.7.cloned.1.call-update) | async-done | bytes 1048592 | tf_op jit(solution)/shard_map/psum | solution.py:161
  115.9 1.4 multiply_reduce_fusion.2
  121.3 1.5 multiply_convert_fusion.1
  123.6 1.6 convolution_add_fusion.2
  125.3 1.2 multiply_multiply_fusion.1
  126.5 35.6 %all-reduce.9.cloned.1.call-done = f32[256,1024]{1,0:T(8,128)} async-done(((f32[256,1024]{1,0:T(8,128)}), f32[256,1024]{1,0:T(8,128)}) %all-reduce.9.cloned.1.call-update) | async-done | bytes 1048592 | tf_op jit(solution)/shard_map/psum | solution.py:182
  162.1 2.2 multiply_reduce_fusion
  164.4 1.1 subtract_add_fusion
  165.6 1.6 fusion.65
  168.0 1.2 convolution_bitcast_fusion.1
  170.1 9.3 %while.60 = (s32[]{:T(128)}, f32[1,128,256]{2,1,0:T(8,128)S(1)}, f32[4,1,128,256]{3,2,1,0:T(8,128)}, f32[4,1,128]{2,1,0:T(1,128)}, f32[4,1,128,256]{3,2,1,0:T(8,128)}, /*index=5*/s32[]{:T(128)}, s32[]{:T(128)}, s32[]{:T(128)}) while((s32[]{:T(128)}, f32[1,128,256]{2,1,0:T(8,128)S(1)}, f32[4,1,128,256]{3,2,1,0:T(8,128)}, ...), condition=%wide.region_15.16_spmd.clone, body=%wide.region_14.15_spmd.clone.sunk | while | flops 131076 | bytes 657016 | solution.py:87
  180.9 2.6 fusion.121
  183.8 1.1 fusion.16
  185.1 1.0 fusion.123
  186.2 1.2 fusion.15
  187.4 33.6 %all-gather.9.cloned.1.call-done = f32[8,128,256]{2,1,0:T(8,128)} async-done(((f32[1,128,256]{2,1,0:T(8,128)}), f32[8,128,256]{2,1,0:T(8,128)}) %all-gather.9.cloned.1.call-update) | async-done | bytes 1048592 | tf_op jit(solution)/shard_map/all_gather | solution.py:20
  221.0 2.3 reverse_bitcast_fusion
  223.3 15.3 %while.61 = (s32[]{:T(128)}, f32[1,128,256]{2,1,0:T(8,128)S(1)}, s32[]{:T(128)}, f32[8,1,128]{2,1,0:T(1,128)}, f32[8,1,128,256]{3,2,1,0:T(8,128)}, /*index=5*/s32[]{:T(128)}, s32[]{:T(128)}) while((s32[]{:T(128)}, f32[1,128,256]{2,1,0:T(8,128)S(1)}, s32[]{:T(128)}, f32[8,1,128]{2,1,0:T(1,128)}, f32[8,1,128,256]{3,2,1,0:T(8,128)}, ...), condition=%wide.region_17.18_spmd.clone, body=%wide.region_16.17_spmd.clone.sunk | while | flops 131076 | bytes 394857 | solution.py:32
  223.3 1.2 dynamic-slice_bitcast_fusion.5
  225.5 1.2 dynamic-slice_bitcast_fusion.5
  227.7 1.2 dynamic-slice_bitcast_fusion.5
  229.8 1.2 dynamic-slice_bitcast_fusion.5
  232.0 1.2 dynamic-slice_bitcast_fusion.5
  234.2 1.2 dynamic-slice_bitcast_fusion.5
  236.4 1.2 dynamic-slice_bitcast_fusion.5
  239.6 1.7 convolution_add_fusion.3
  243.6 1.0 multiply_reduce_fusion.5
  245.4 1.3 collective-permute-start.1
  247.7 3.2 collective-permute-done.1
  250.9 2.1 fusion.42
  253.0 1.7 fusion.33
  255.5 1.3 convolution_add_fusion
  256.8 61.0 %all-reduce.11.cloned.1.call-done = f32[1024,16]{0,1:T(8,128)} async-done(((f32[1024,16]{0,1:T(8,128)}), f32[1024,16]{0,1:T(8,128)}) %all-reduce.11.cloned.1.call-update) | async-done | bytes 65552 | tf_op jit(solution)/shard_map/psum | solution.py:263
  317.9 1.9 convolution_bitcast_fusion
  320.6 2.5 fusion.70
  323.3 2.4 fusion.105
  325.7 3.1 fusion.124
  328.9 3.1 fusion.125
  333.1 3.2 fusion.51
  337.2 35.4 %all-reduce.13.cloned.1.call-done = (f32[256,1024]{1,0:T(8,128)}, f32[256,1024]{1,0:T(8,128)}, f32[1024,16]{0,1:T(8,128)}) async-done(((f32[256,1024]{1,0:T(8,128)}, f32[256,1024]{1,0:T(8,128)}, f32[1024,16]{0,1:T(8,128)}), (f32[256,1024]{1,0:T(8,128)}, f32[256,1024]{1,0:T(8,128)}, f32[1024,16]{0,1:T(8,128)})) %all-reduce.13.cloned.1.call-update) | async-done | bytes 2162704 | tf_op jit(solution)/shard_map/psum | solution.py:168
  372.6 1.5 fusion.30
  374.2 38.0 %all-reduce = (f32[1024]{0:T(1024)}, f32[4,1,512]{2,1,0:T(1,128)}, f32[16,128]{1,0:T(8,128)}, f32[128]{0:T(128)}, f32[256]{0:T(256)S(1)}, /*index=5*/f32[1024]{0:T(1024)}) all-reduce(f32[1024]{0:T(1024)S(1)} %get-tuple-element.475, f32[4,1,512]{2,1,0:T(1,128)S(1)} %reshape.447, ...), channel_id=1, replica_groups=mesh['seq'=8,'head'=4] {'seq'}, use_global_device_ids=true, to_apply=%region_22.23 | all-reduce | flops 6528 | bytes 52224 | tf_op jit(solution)/shard_map/psum | solution.py:262
  412.2 6.4 psum.102
  418.7 3.5 fusion.27
  422.1 22.5 %reduce-scatter.7.cloned.1.call-done = f32[128,1,512]{2,0,1:T(8,128)} async-done(((f32[1024,1,512]{2,0,1:T(8,128)}), f32[128,1,512]{2,0,1:T(8,128)}) %reduce-scatter.7.cloned.1.call-update) | async-done | bytes 262160 | tf_op jit(solution)/shard_map/reduce_scatter | solution.py:257
  444.6 1.9 copy.47
  446.5 65.8 %reduce-scatter.11.cloned.1.call-done = f32[256,128]{1,0:T(8,128)} async-done(((f32[256,1024]{1,0:T(8,128)}), f32[256,128]{1,0:T(8,128)}) %reduce-scatter.11.cloned.1.call-update) | async-done | bytes 131088 | tf_op jit(solution)/shard_map/reduce_scatter | solution.py:259
  512.3 67.1 %reduce-scatter.9.cloned.1.call-done = f32[128,256]{1,0:T(8,128)} async-done(((f32[1024,256]{1,0:T(8,128)}), f32[128,256]{1,0:T(8,128)}) %reduce-scatter.9.cloned.1.call-update) | async-done | bytes 131088 | tf_op jit(solution)/shard_map/reduce_scatter | solution.py:258
  579.4 76.0 %reduce-scatter.13.cloned.1.call-done = f32[128,704]{0,1:T(8,128)} async-done(((f32[1024,704]{0,1:T(8,128)}), f32[128,704]{0,1:T(8,128)}) %reduce-scatter.13.cloned.1.call-update) | async-done | bytes 360464 | tf_op jit(solution)/shard_map/reduce_scatter | solution.py:178
  655.4 76.3 %reduce-scatter.15.cloned.1.call-done = f32[128,704]{0,1:T(8,128)} async-done(((f32[1024,704]{0,1:T(8,128)}), f32[128,704]{0,1:T(8,128)}) %reduce-scatter.15.cloned.1.call-update) | async-done | bytes 360464 | tf_op jit(solution)/shard_map/reduce_scatter | solution.py:179
  731.7 76.1 %reduce-scatter.17.cloned.1.call-done = f32[704,128]{1,0:T(8,128)} async-done(((f32[704,1024]{1,0:T(8,128)}), f32[704,128]{1,0:T(8,128)}) %reduce-scatter.17.cloned.1.call-update) | async-done | bytes 360464 | tf_op jit(solution)/shard_map/reduce_scatter | solution.py:180
  (305 shorter events, 50.4 us)
Async XLA Ops:
  7.2 113.6 %copy-start = (bf16[704,1024]{1,0:T(8,128)(2,1)S(1)}, bf16[704,1024]{1,0:T(8,128)(2,1)}, u32[]{:S(2)}) copy-start(bf16[704,1024]{1,0:T(8,128)(2,1)} %param.37) | copy-start | bytes 4325380
  7.2 8.9 %copy-start.3 = (bf16[1,256,1024]{2,1,0:T(8,128)(2,1)S(1)}, bf16[1,256,1024]{2,1,0:T(8,128)(2,1)}, u32[]{:S(2)}) copy-start(bf16[1,256,1024]{2,1,0:T(8,128)(2,1)} %param.23) | copy-start | bytes 1572868
  7.2 8.9 %copy-start.54 = (f32[1024]{0:T(1024)S(1)}, f32[1024]{0:T(1024)}, u32[]{:S(2)}) copy-start(f32[1024]{0:T(1024)} %param.25) | copy-start | bytes 12292
  7.2 8.9 %copy-start.56 = (bf16[1024,16]{0,1:T(8,128)(2,1)S(1)}, bf16[1024,16]{0,1:T(8,128)(2,1)}, u32[]{:S(2)}) copy-start(bf16[1024,16]{0,1:T(8,128)(2,1)} %param.28) | copy-start | bytes 98308
  7.2 60.5 %all-gather.7.cloned.1.call-start = ((), (), s32[]{:S(2)}) async-start(), calls=%async_computation.15 | async-start | bytes 1179648 | tf_op jit(solution)/shard_map/all_gather | solution.py:20
  9.2 7.2 copy-start.84
  9.2 7.2 copy-start.92
  9.2 8.2 %copy-start.82 = (f32[4,1,512]{2,1,0:T(1,128)S(1)}, f32[4,1,512]{2,1,0:T(1,128)}, u32[]{:S(2)}) copy-start(f32[4,1,512]{2,1,0:T(1,128)} %param.27) | copy-start | bytes 24580
  11.1 7.4 copy-start.8
  11.2 6.3 collective-permute-start
  18.7 49.0 %copy-start.12 = (f32[1,256,128]{2,1,0:T(8,128)}, f32[1,256,128]{2,1,0:T(8,128)S(1)}, u32[]{:S(2)}) copy-start(f32[1,256,128]{2,1,0:T(8,128)S(1)} %slice.81) | copy-start | bytes 393220
  18.7 29.7 %copy-start.19 = (bf16[1,256,256]{2,1,0:T(8,128)(2,1)}, bf16[1,256,256]{2,1,0:T(8,128)(2,1)S(1)}, u32[]{:S(2)}) copy-start(bf16[1,256,256]{2,1,0:T(8,128)(2,1)S(1)} %slice.82) | copy-start | bytes 393220
  19.0 148.4 %copy-start.24 = (f32[1,4,64,128]{3,2,1,0:T(8,128)}, f32[1,4,64,128]{3,2,1,0:T(8,128)S(1)}, u32[]{:S(2)}) copy-start(f32[1,4,64,128]{3,2,1,0:T(8,128)S(1)} %get-tuple-element.560) | copy-start | bytes 393220
  24.6 50.9 %copy-start.16 = (f32[4,1,128,256]{3,2,1,0:T(8,128)}, f32[4,1,128,256]{3,2,1,0:T(8,128)S(1)}, u32[]{:S(2)}) copy-start(f32[4,1,128,256]{3,2,1,0:T(8,128)S(1)} %get-tuple-element.335) | copy-start | bytes 1572868
  25.3 90.6 %all-reduce.7.cloned.1.call-start = ((), (), s32[]{:S(2)}) async-start(), calls=%async_computation.6 | async-start | bytes 2097152 | tf_op jit(solution)/shard_map/psum | solution.py:161
  25.4 42.3 %copy-start.47 = (f32[64,64]{1,0:T(8,128)}, f32[64,64]{1,0:T(8,128)S(1)}, u32[]{:S(2)}) copy-start(f32[64,64]{1,0:T(8,128)S(1)} %fusion.102) | copy-start | bytes 49156
  48.1 27.4 %copy-start.61 = (f32[4,128]{1,0:T(4,128)}, f32[4,128]{1,0:T(4,128)S(1)}, u32[]{:S(2)}) copy-start(f32[4,128]{1,0:T(4,128)S(1)} %get-tuple-element.551) | copy-start | bytes 6148
  48.5 28.6 %copy-start.35 = (f32[4,64,64]{2,1,0:T(8,128)}, f32[4,64,64]{2,1,0:T(8,128)S(1)}, u32[]{:S(2)}) copy-start(f32[4,64,64]{2,1,0:T(8,128)S(1)} %convolution_multiply_fusion.1) | copy-start | bytes 196612
  67.7 9.6 %copy-start.88 = (f32[256]{0:T(256)S(1)}, f32[256]{0:T(256)}, u32[]{:S(2)}) copy-start(f32[256]{0:T(256)} %param.32) | copy-start | bytes 3076
  77.1 2.3 copy-start.37
  77.2 2.2 copy-start.75
  80.7 37.2 %copy-start.55 = (f32[1024]{0:T(1024)S(1)}, f32[1024]{0:T(1024)}, u32[]{:S(2)}) copy-start(f32[1024]{0:T(1024)} %param.34) | copy-start | bytes 12292
  80.7 81.4 %all-reduce.9.cloned.1.call-start = ((), (), s32[]{:S(2)}) async-start(), calls=%async_computation.7 | async-start | bytes 2097152 | tf_op jit(solution)/shard_map/psum | solution.py:182
  125.2 95.8 %all-gather.9.cloned.1.call-start = ((), (), s32[]{:S(2)}) async-start(), calls=%async_computation.16 | async-start | bytes 1179648 | tf_op jit(solution)/shard_map/all_gather | solution.py:20
  162.1 2.2 copy-start.18
  162.1 2.2 copy-start.29
  170.1 10.2 %copy-start.74 = (f32[8,1,128]{2,1,0:T(1,128)S(1)}, f32[8,1,128]{2,1,0:T(1,128)}, u32[]{:S(2)}) copy-start(f32[8,1,128]{2,1,0:T(1,128)} %copy-done.73) | copy-start | bytes 12292
  180.1 3.5 copy-start.20
  180.1 137.7 %all-reduce.11.cloned.1.call-start = ((), (), s32[]{:S(2)}) async-start(), calls=%async_computation.9 | async-start | bytes 131072 | tf_op jit(solution)/shard_map/psum | solution.py:263
  180.9 2.7 copy-start.23
  180.9 2.7 copy-start.48
  180.9 2.9 copy-start.25
  180.9 3.9 copy-start.13
  183.6 2.6 copy-start.17
  183.6 2.6 copy-start.62
  223.3 15.4 %copy-start.2 = (f32[1,128,256]{2,1,0:T(8,128)S(1)}, f32[1,128,256]{2,1,0:T(8,128)}, u32[]{:S(2)}) copy-start(f32[1,128,256]{2,1,0:T(8,128)} %copy-done.1) | copy-start | bytes 393220
  223.3 16.3 %copy-start.60 = (f32[4,128]{1,0:T(4,128)S(1)}, f32[4,128]{1,0:T(4,128)}, u32[]{:S(2)}) copy-start(f32[4,128]{1,0:T(4,128)} %get-tuple-element.550) | copy-start | bytes 6148
  238.6 2.8 copy-start.14
  238.6 2.8 copy-start.15
  238.6 2.8 copy-start.21
  238.6 2.8 copy-start.34
  238.6 2.8 copy-start.39
  238.6 2.8 copy-start.40
  239.6 2.4 copy-start.93
  243.5 7.4 copy-start.64
  243.5 7.4 copy-start.66
  243.5 7.4 copy-start.68
  243.5 7.4 copy-start.70
  245.4 5.5 collective-permute-start.1
  247.6 7.1 copy-start.46
  247.6 125.0 %all-reduce.13.cloned.1.call-start = ((), (), s32[]{:S(2)}) async-start(), calls=%async_computation.17 | async-start | bytes 4325376 | tf_op jit(solution)/shard_map/psum | solution.py:168
  247.7 7.0 copy-start.43
  317.8 126.8 %reduce-scatter.7.cloned.1.call-start = ((), (), s32[]{:S(2)}) async-start(), calls=%async_computation.8 | async-start | bytes 2359296 | tf_op jit(solution)/shard_map/reduce_scatter | solution.py:257
  319.8 192.6 %reduce-scatter.11.cloned.1.call-start = ((), (), s32[]{:S(2)}) async-start(), calls=%async_computation.11 | async-start | bytes 1179648 | tf_op jit(solution)/shard_map/reduce_scatter | solution.py:259
  323.2 2.5 copy-start.6
  323.2 256.2 %reduce-scatter.9.cloned.1.call-start = ((), (), s32[]{:S(2)}) async-start(), calls=%async_computation.10 | async-start | bytes 1179648 | tf_op jit(solution)/shard_map/reduce_scatter | solution.py:258
  325.7 329.8 %reduce-scatter.13.cloned.1.call-start = ((), (), s32[]{:S(2)}) async-start(), calls=%async_computation.12 | async-start | bytes 3244032 | tf_op jit(solution)/shard_map/reduce_scatter | solution.py:178
  328.8 402.9 %reduce-scatter.15.cloned.1.call-start = ((), (), s32[]{:S(2)}) async-start(), calls=%async_computation.13 | async-start | bytes 3244032 | tf_op jit(solution)/shard_map/reduce_scatter | solution.py:179
  332.1 475.8 %reduce-scatter.17.cloned.1.call-start = ((), (), s32[]{:S(2)}) async-start(), calls=%async_computation.14 | async-start | bytes 3244032 | tf_op jit(solution)/shard_map/reduce_scatter | solution.py:180
  336.3 37.9 %copy-start.72 = (f32[1024]{0:T(1024)S(1)}, f32[1024]{0:T(1024)}, u32[]{:S(2)}) copy-start(f32[1024]{0:T(1024)} %get-tuple-element.473) | copy-start | bytes 12292
  336.3 37.9 %copy-start.90 = (f32[256]{0:T(256)S(1)}, f32[256]{0:T(256)}, u32[]{:S(2)}) copy-start(f32[256]{0:T(256)} %get-tuple-element.480) | copy-start | bytes 3076
  336.3 37.9 %copy-start.91 = (f32[128]{0:T(128)S(1)}, f32[128]{0:T(128)}, u32[]{:S(2)}) copy-start(f32[128]{0:T(128)} %get-tuple-element.568) | copy-start | bytes 1540
  336.3 82.3 %copy-start.86 = (f32[256]{0:T(256)S(1)}, f32[256]{0:T(256)}, u32[]{:S(2)}) copy-start(f32[256]{0:T(256)} %get-tuple-element.552) | copy-start | bytes 3076
  418.7 389.2 %copy-start.53 = (f32[1024,16]{0,1:T(8,128)S(1)}, f32[1024,16]{0,1:T(8,128)}, u32[]{:S(2)}) copy-start(f32[1024,16]{0,1:T(8,128)} %get-tuple-element.790) | copy-start | bytes 196612
  (44 other events, 51.2 us)
Sparse Core Ops, SparseCore 0:
  25.4 42.2 all-gather.6
  80.8 34.9 all-reduce.6
  125.3 36.7 all-reduce.8
  180.2 40.7 all-gather.8
  247.7 70.0 all-reduce.10
  320.2 52.4 all-reduce.12
  376.2 68.4 reduce-scatter.6
  448.6 63.6 reduce-scatter.10
  516.3 63.0 reduce-scatter.8
  583.4 71.9 reduce-scatter.12
  659.6 72.0 reduce-scatter.14
  735.7 72.0 reduce-scatter.16
